TPU v7x, 256 devices: a whole 4x4x8 slice. The times are simulated.
256 devices in a mesh: slab: 32 (over z, y), snap: 8 (over x, core).
Axes of the slice: x: 4, y: 4, z: 8, core: 2. Of those that a mesh axis runs over, the one named last changes fastest.
Arguments:
- flow: bfloat16 [128, 3, 64, 64, 128], P('snap', None, 'slab'), may hold values from -127 to 127
- large_scale: bfloat16 [3, 64, 64, 128], P(None, 'slab'), may hold values from -6 to 6
- modulation: float32 [128, 64], replicated, may hold values from -15 to 15
- metric: float32 [4, 64, 64, 128], P(None, 'slab'), may hold values from -0.5 to 9.6
Outputs:
- whitened: float32 [128, 3, 64, 64, 128], P(None, None, 'slab', 'snap')
All inputs are finite; a program needn't handle non-finite values.
Results may differ from a plain program's by a relative error of at most 0.0003.
Values may be sent and summed in bfloat16 or wider, within the bound.
A program may use at most 64 MiB of HBM per device.

v0:
```python
import jax
import jax.numpy as jnp
from jax import lax
from jax.sharding import PartitionSpec as P

NSITER = 6


def with_halo(block, sides, width):
    for axis, dim in sides:
        count = lax.axis_size(axis)
        forward = [(i, i + 1) for i in range(count - 1)]
        backward = [(target, source) for source, target in forward]
        low = lax.ppermute(
            lax.slice_in_dim(block, block.shape[dim] - width, None, axis=dim), axis, forward
        )
        high = lax.ppermute(lax.slice_in_dim(block, 0, width, axis=dim), axis, backward)
        block = jnp.concatenate([low, block, high], axis=dim)
    return block


def vorticity(velocity, metric):
    metric_x = metric[0]
    shear_xy = metric[1]
    metric_y = metric[2]
    metric_z = metric[3]

    def along_x(values):
        return 0.5 * (values[..., 1:-1, 2:, :] - values[..., 1:-1, :-2, :])

    def along_y(values):
        return 0.5 * (values[..., 2:, 1:-1, :] - values[..., :-2, 1:-1, :])

    def along_z(values):
        center = values[..., 1:-1, 1:-1, :]
        return 0.5 * (jnp.roll(center, -1, -1) - jnp.roll(center, 1, -1))

    def slope_x(values):
        return metric_x * along_x(values) + shear_xy * along_y(values)

    def slope_y(values):
        return metric_y * along_y(values)

    def slope_z(values):
        return metric_z * along_z(values)

    stream = velocity[..., 0, :, :, :]
    normal = velocity[..., 1, :, :, :]
    spanwise = velocity[..., 2, :, :, :]
    around_x = slope_y(spanwise) - slope_z(normal)
    around_y = slope_z(stream) - slope_x(spanwise)
    around_z = slope_x(normal) - slope_y(stream)
    return jnp.stack([around_x, around_y, around_z], axis=-4)


def wrap_columns(values):
    return jnp.concatenate([values[..., -1:, :], values, values[..., :1, :]], axis=-2)


def whitening(correlation):
    identity = jnp.eye(correlation.shape[0], dtype=correlation.dtype)
    frob_scale = jnp.sqrt(jnp.sum(correlation * correlation) + 1e-06)
    approx = correlation / frob_scale
    inverse = identity
    for repeat in range(NSITER):
        factor = 0.5 * (3.0 * identity - jnp.dot(inverse, approx, precision=lax.Precision.HIGHEST))
        approx = jnp.dot(approx, factor, precision=lax.Precision.HIGHEST)
        inverse = jnp.dot(factor, inverse, precision=lax.Precision.HIGHEST)
    return inverse / jnp.sqrt(frob_scale)


def inner_rows(left_rows, right_rows):
    return lax.dot_general(
        left_rows,
        right_rows,
        (((1,), (1,)), ((), ())),
        precision=lax.Precision.HIGHEST,
        preferred_element_type=jnp.float32,
    )


def planes_padded(flow, large_scale):
    joined = jnp.concatenate([flow, large_scale[None]], axis=0)
    return with_halo(joined, (("slab", 2),), 1)


def per_device(flow, large_scale, modulation, metric):
    snap_count = lax.axis_size("snap")
    slab_count = lax.axis_size("slab")
    own_snaps = flow.shape[0]
    block_cols = flow.shape[3] // snap_count
    snap_index = lax.axis_index("snap")
    mod_ext = jnp.concatenate([modulation[:, -1:], modulation, modulation[:, :1]], axis=1)
    padded = planes_padded(flow, large_scale)
    large_ext = wrap_columns(padded[own_snaps].astype(jnp.float32))
    mod_mine = lax.dynamic_slice_in_dim(mod_ext, snap_index * own_snaps, own_snaps, 0)
    velocity = (
        wrap_columns(padded[:own_snaps].astype(jnp.float32))
        + mod_mine[:, None, None, :, None] * large_ext[None]
    )
    local_fields = vorticity(velocity, metric)
    pieces = local_fields.reshape(
        own_snaps, 3, local_fields.shape[2], snap_count, block_cols, local_fields.shape[4]
    )
    fields = lax.all_to_all(pieces, "snap", split_axis=3, concat_axis=0, tiled=True)[:, :, :, 0]
    snapshot_rows = fields.reshape(fields.shape[0], -1)
    gram_local = inner_rows(snapshot_rows, snapshot_rows)
    gram_total = lax.psum(gram_local, ("slab", "snap"))
    correlation = gram_total / (snapshot_rows.shape[1] * slab_count * snap_count)
    weights = whitening(correlation)
    result = jnp.dot(weights, snapshot_rows, precision=lax.Precision.HIGHEST)
    return result.reshape(fields.shape)


def solution(mesh):
    return jax.shard_map(
        per_device,
        mesh=mesh,
        in_specs=(
            P("snap", None, "slab", None, None),
            P(None, "slab", None, None),
            P(),
            P(None, "slab", None, None),
        ),
        out_specs=P(None, None, "slab", "snap", None),
        check_vma=False,
    )
```

profile of v0, /device:TPU:1, one launch (start us, length us, event | category | flops | bytes accessed | tf_op | source)
XLA Modules:
  0.0 358.1 jit_solution(2387422955889473556)
XLA Ops:
  6.5 2.9 fusion.21
  9.4 4.1 %collective-permute-start = (bf16[17,3,1,64,128]{4,3,2,1,0:T(8,128)(2,1)}, bf16[17,3,1,64,128]{4,3,2,1,0:T(8,128)(2,1)S(1)}, u32[]{:S(2)}, u32[]{:S(2)}) collective-permute-start(bf16[17,3,1,64,128]{4,3,2,1,0:T(8,128)(2,1)} %get-tuple-element.20), channel_id=1, source_target_pairs={{0,8},{8,16},{16,24},{24,32},{32,40},{40,48},{48,56},{56,64},{64,7... | collective-permute-start | bytes 2506760 | tf_op jit(solution)/shard_map/ppermute | solution.py:14
  13.5 1.3 collective-permute-start.1
  15.0 1.0 multiply_bitcast_fusion.2
  15.9 15.1 %collective-permute-done = bf16[17,3,1,64,128]{4,3,2,1,0:T(8,128)(2,1)S(1)} collective-permute-done((bf16[17,3,1,64,128]{4,3,2,1,0:T(8,128)(2,1)}, bf16[17,3,1,64,128]{4,3,2,1,0:T(8,128)(2,1)S(1)}, u32[]{:S(2)}, u32[]{:S(2)}) %collective-permute-start) | collective-permute-done | bytes 835616 | tf_op jit(solution)/shard_map/ppermute | solution.py:14
  31.0 3.8 %collective-permute-done.1 = bf16[17,3,1,64,128]{4,3,2,1,0:T(8,128)(2,1)S(1)} collective-permute-done((bf16[17,3,1,64,128]{4,3,2,1,0:T(8,128)(2,1)}, bf16[17,3,1,64,128]{4,3,2,1,0:T(8,128)(2,1)S(1)}, u32[]{:S(2)}, u32[]{:S(2)}) %collective-permute-start.1) | collective-permute-done | bytes 835616 | tf_op jit(solution)/shard_map/ppermute | solution.py:17
  34.8 0.5 pad_maximum_fusion
  35.3 0.7 slice_convert_fusion
  36.3 1.5 maximum_add_fusion
  37.7 0.5 slice_bitcast_fusion.2
  38.2 0.9 fusion.28
  39.1 0.9 fusion.29
  40.0 0.8 fusion.9
  40.7 1.5 fusion.19
  42.8 43.4 %all_to_all.15 = f32[16,3,2,8,8,128]{5,4,2,1,0,3:T(8,128)} all-to-all(f32[16,3,2,8,8,128]{5,4,2,1,0,3:T(8,128)S(1)} %copy.19), channel_id=1, replica_groups=mesh['slab'=32,'snap'=8] {'snap'}, dimensions={3} | all-to-all | bytes 6291456 | tf_op jit(solution)/shard_map/all_to_all | solution.py:105
  86.2 2.8 reshape_squeeze.3
  89.0 3.2 fusion.34
  92.2 2.4 copy.16
  94.6 242.7 %all-reduce.2.cloned.1.call-done = f32[128,128]{1,0:T(8,128)} async-done(((f32[128,128]{1,0:T(8,128)}), f32[128,128]{1,0:T(8,128)}) %all-reduce.2.cloned.1.call-update) | async-done | bytes 65552 | tf_op jit(solution)/shard_map/psum | solution.py:108
  337.3 1.5 multiply_reduce_fusion
  339.5 1.0 fusion.6
  340.7 1.0 fusion.24
  344.7 3.0 fusion.43
  347.8 3.5 copy.17
  (34 shorter events, 4.0 us)
Async XLA Ops:
  6.5 28.2 %copy-start = (bf16[16,3,2,64,128]{4,3,2,1,0:T(8,128)(2,1)S(1)}, bf16[16,3,2,64,128]{4,3,2,1,0:T(8,128)(2,1)}, u32[]{:S(2)}) copy-start(bf16[16,3,2,64,128]{4,3,2,1,0:T(8,128)(2,1)} %param.4) | copy-start | bytes 4718596
  6.5 28.2 %copy-start.2 = (bf16[3,2,64,128]{3,2,1,0:T(8,128)(2,1)S(1)}, bf16[3,2,64,128]{3,2,1,0:T(8,128)(2,1)}, u32[]{:S(2)}) copy-start(bf16[3,2,64,128]{3,2,1,0:T(8,128)(2,1)} %param.5) | copy-start | bytes 294916
  6.5 8.2 %copy-start.3 = (f32[128,64]{0,1:T(8,128)S(1)}, f32[128,64]{0,1:T(8,128)}, u32[]{:S(2)}) copy-start(f32[128,64]{0,1:T(8,128)} %param.6) | copy-start | bytes 98308
  6.5 330.8 %all-reduce.2.cloned.1.call-start = ((), (), s32[]{:S(2)}) async-start(), calls=%async_computation.1 | async-start | bytes 131072 | tf_op jit(solution)/shard_map/psum | solution.py:108
  9.4 21.6 %collective-permute-start = (bf16[17,3,1,64,128]{4,3,2,1,0:T(8,128)(2,1)}, bf16[17,3,1,64,128]{4,3,2,1,0:T(8,128)(2,1)S(1)}, u32[]{:S(2)}, u32[]{:S(2)}) collective-permute-start(bf16[17,3,1,64,128]{4,3,2,1,0:T(8,128)(2,1)} %get-tuple-element.20), channel_id=1, source_target_pairs={{0,8},{8,16},{16,24},{24,32},{32,40},{40,48},{48,56},{56,64},{64,7... | collective-permute-start | bytes 2506760 | tf_op jit(solution)/shard_map/ppermute | solution.py:14
  13.5 21.3 %collective-permute-start.1 = (bf16[17,3,1,64,128]{4,3,2,1,0:T(8,128)(2,1)}, bf16[17,3,1,64,128]{4,3,2,1,0:T(8,128)(2,1)S(1)}, u32[]{:S(2)}, u32[]{:S(2)}) collective-permute-start(bf16[17,3,1,64,128]{4,3,2,1,0:T(8,128)(2,1)} %get-tuple-element.21), channel_id=1, source_target_pairs={{8,0},{16,8},{24,16},{32,24},{40,32},{48,40},{56,48},{64,56},{72,6... | collective-permute-start | bytes 2506760 | tf_op jit(solution)/shard_map/ppermute | solution.py:17
  94.6 250.2 %copy-start.1 = (f32[6144,128]{1,0:T(8,128)S(1)}, f32[6144,128]{1,0:T(8,128)}, u32[]{:S(2)}) copy-start(f32[6144,128]{1,0:T(8,128)} %copy.16) | copy-start | bytes 9437188
Sparse Core Ops, SparseCore 0:
  92.3 244.9 all-reduce.1
where the time goes:
time: 358 us
  waiting for transfers between devices  262 us (73%)
  blocking collectives  43.4 us (12%)
  between operations  14.4 us (4%)
  local copies, waits for them, and re-layouts  11.3 us (3%)
  matrix products  11.3 us (3%)
  other arithmetic  10.6 us (3%)
  starting transfers between devices  5.35 us (1%)
    psum x1, waiting for transfers between devices, per_device(): gram_total = lax.psum(gram_local, ('slab', 'snap'))  243 us
    all_to_all x1, blocking collectives, per_device(): lax.all_to_all(pieces, 'snap', split_axis=3, concat_axis=0, tiled=True)  43.4 us
    ppermute x1, waiting for transfers between devices, with_halo(): lax.ppermute(lax.slice_in_dim(block, block.shape[dim] - width, None, axis...  15.1 us
  transfers between devices with their start and end apart: 3, of which 3 were waited for; matrix products, arithmetic and copies ran while one was open for 1% of the time, Pallas kernels for 0%

commit v1 on v0

--- a/solution.py
+++ b/solution.py
@@ -105,7 +105,7 @@
     fields = lax.all_to_all(pieces, "snap", split_axis=3, concat_axis=0, tiled=True)[:, :, :, 0]
     snapshot_rows = fields.reshape(fields.shape[0], -1)
     gram_local = inner_rows(snapshot_rows, snapshot_rows)
-    gram_total = lax.psum(gram_local, ("slab", "snap"))
+    gram_total = jnp.sum(lax.all_gather(gram_local, ("slab", "snap")), axis=0)
     correlation = gram_total / (snapshot_rows.shape[1] * slab_count * snap_count)
     weights = whitening(correlation)
     result = jnp.dot(weights, snapshot_rows, precision=lax.Precision.HIGHEST)

time: 358 us -> 247 us (0.69)
  waiting for transfers between devices: 262 us -> 145 us
  other arithmetic: 10.6 us -> 16.4 us
    psum x1 -> x0, waiting for transfers between devices: 243 us -> none  [per_device(): gram_total = lax.psum(gram_local, ('slab', 'snap'))]
    all_gather x0 -> x1, waiting for transfers between devices: none -> 127 us  [per_device(): gram_total = jnp.sum(lax.all_gather(gram_local, ('slab', 'snap')), axis=0)]
    reduce_sum x0 -> x1, other arithmetic: none -> 6.59 us  [per_device(): gram_total = jnp.sum(lax.all_gather(gram_local, ('slab', 'snap')), axis=0)]
where the time goes in v1:
time: 247 us; the launch traced here: 246 us
  waiting for transfers between devices  145 us (59%)
  blocking collectives  43.4 us (18%)
  other arithmetic  16.4 us (7%)
  between operations  14.7 us (6%)
  local copies, waits for them, and re-layouts  11.3 us (5%)
  matrix products  9.65 us (4%)
  starting transfers between devices  5.35 us (2%)
    all_gather x1, waiting for transfers between devices, per_device(): gram_total = jnp.sum(lax.all_gather(gram_local, ('slab', 'snap')), axis=0)  127 us
    all_to_all x1, blocking collectives, per_device(): lax.all_to_all(pieces, 'snap', split_axis=3, concat_axis=0, tiled=True)  43.4 us
    ppermute x1, waiting for transfers between devices, with_halo(): lax.ppermute(lax.slice_in_dim(block, block.shape[dim] - width, None, axis...  15.1 us
    reduce_sum x1, other arithmetic, per_device(): gram_total = jnp.sum(lax.all_gather(gram_local, ('slab', 'snap')), axis=0)  6.59 us
    dot_general x2, local copies, waits for them, and re-layouts, per_device(): result = jnp.dot(weights, snapshot_rows, precision=lax.Precision.HIGHEST)  5.85 us
  transfers between devices with their start and end apart: 3, of which 3 were waited for; matrix products, arithmetic and copies ran while one was open for 1% of the time, Pallas kernels for 0%

profile of v1, /device:TPU:1, one launch (start us, length us, event | category | flops | bytes accessed | tf_op | source)
XLA Modules:
  0.0 246.4 jit_solution(129712450595528247)
XLA Ops:
  6.5 2.9 %fusion.21 = (bf16[17,3,1,64,128]{4,3,2,1,0:T(8,128)(2,1)}, bf16[17,3,1,64,128]{4,3,2,1,0:T(8,128)(2,1)}) fusion(bf16[16,3,2,64,128]{4,3,2,1,0:T(8,128)(2,1)} %param.4, bf16[1,3,2,64,128]{4,3,2,1,0:T(8,128)(2,1)} %bitcast.82), kind=kLoop, calls=%fused_computation.44 | loop fusion | flops 835584 | bytes 3342336 | tf_op jit(solution)/shard_map/concatenate | solution.py:83
  9.4 4.1 %collective-permute-start = (bf16[17,3,1,64,128]{4,3,2,1,0:T(8,128)(2,1)}, bf16[17,3,1,64,128]{4,3,2,1,0:T(8,128)(2,1)S(1)}, u32[]{:S(2)}, u32[]{:S(2)}) collective-permute-start(bf16[17,3,1,64,128]{4,3,2,1,0:T(8,128)(2,1)} %get-tuple-element.20), channel_id=1, source_target_pairs={{0,8},{8,16},{16,24},{24,32},{32,40},{40,48},{48,56},{56,64},{64,7... | collective-permute-start | bytes 2506760 | tf_op jit(solution)/shard_map/ppermute | solution.py:14
  13.5 1.3 collective-permute-start.1
  15.0 1.0 multiply_bitcast_fusion.2
  15.9 15.1 %collective-permute-done = bf16[17,3,1,64,128]{4,3,2,1,0:T(8,128)(2,1)S(1)} collective-permute-done((bf16[17,3,1,64,128]{4,3,2,1,0:T(8,128)(2,1)}, bf16[17,3,1,64,128]{4,3,2,1,0:T(8,128)(2,1)S(1)}, u32[]{:S(2)}, u32[]{:S(2)}) %collective-permute-start) | collective-permute-done | bytes 835616 | tf_op jit(solution)/shard_map/ppermute | solution.py:14
  31.0 3.8 %collective-permute-done.1 = bf16[17,3,1,64,128]{4,3,2,1,0:T(8,128)(2,1)S(1)} collective-permute-done((bf16[17,3,1,64,128]{4,3,2,1,0:T(8,128)(2,1)}, bf16[17,3,1,64,128]{4,3,2,1,0:T(8,128)(2,1)S(1)}, u32[]{:S(2)}, u32[]{:S(2)}) %collective-permute-start.1) | collective-permute-done | bytes 835616 | tf_op jit(solution)/shard_map/ppermute | solution.py:17
  34.8 0.5 pad_maximum_fusion
  35.3 0.7 slice_convert_fusion
  36.3 1.5 maximum_add_fusion
  37.7 0.5 slice_bitcast_fusion.2
  38.2 0.9 fusion.28
  39.1 0.9 fusion.29
  40.0 0.8 fusion.9
  40.7 1.5 fusion.19
  42.5 0.3 copy.27
  42.8 43.4 %all_to_all.15 = f32[16,3,2,8,8,128]{5,4,2,1,0,3:T(8,128)} all-to-all(f32[16,3,2,8,8,128]{5,4,2,1,0,3:T(8,128)S(1)} %copy.27), channel_id=1, replica_groups=mesh['slab'=32,'snap'=8] {'snap'}, dimensions={3} | all-to-all | bytes 6291456 | tf_op jit(solution)/shard_map/all_to_all | solution.py:105
  86.2 2.8 %reshape_squeeze.3 = f32[128,6144]{1,0:T(8,128)S(1)} reshape(f32[8,16,3,2,1,8,128]{6,5,3,2,1,0,4:T(8,128)} %bitcast.81) | data formatting | bytes 6291456 | tf_op jit(solution)/shard_map/reshape;squeeze | solution.py:106
  89.0 3.2 %fusion.34 = f32[128,128]{1,0:T(8,128)} fusion(f32[128,6144]{1,0:T(8,128)S(1)} %reshape_squeeze.3), kind=kOutput, calls=%fused_computation.69 | convolution fusion | flops 1207959552 | bytes 3211264 | tf_op jit(solution)/shard_map/dot_general | solution.py:73
  92.2 2.4 copy.24
  94.6 126.6 %all-gather.3.cloned.1.call-done = f32[32768,128]{1,0:T(8,128)} async-done(((f32[128,128]{1,0:T(8,128)}), f32[32768,128]{1,0:T(8,128)}) %all-gather.3.cloned.1.call-update) | async-done | bytes 16777232 | tf_op jit(solution)/shard_map/all_gather | solution.py:108
  221.2 6.6 %reduce_sum.18 = f32[128,128]{1,0:T(8,128)S(1)} reduce(f32[256,128,128]{2,1,0:T(8,128)} %bitcast.79, f32[]{:T(128)} %constant.10.clone.1), dimensions={0}, to_apply=%region_0.1 | reduce | flops 4177920 | bytes 16842756 | tf_op jit(solution)/shard_map/reduce_sum | solution.py:108
  227.8 0.6 multiply_reduce_fusion
  233.0 3.0 %fusion.43 = f32[128,3,2,8,128]{4,0,3,2,1:T(8,128)S(1)} fusion(f32[128,128,1,1,1]{1,0,4,3,2:T(8,128)S(1)} %fusion, f32[3,2,8,128,128]{4,3,2,1,0:T(8,128)S(1)} %bitcast.80), kind=kOutput, calls=%fused_computation.78 | convolution fusion | flops 1207959552 | bytes 6356992 | tf_op jit(solution)/shard_map/dot_general | solution.py:111
  236.0 3.5 %copy.25 = f32[128,3,2,8,128]{4,3,2,1,0:T(8,128)} copy(f32[128,3,2,8,128]{4,0,3,2,1:T(8,128)S(1)} %fusion.43) | data formatting | bytes 6291456 | tf_op jit(solution)/shard_map/dot_general | solution.py:111
  (35 shorter events, 4.1 us)
Async XLA Ops:
  6.5 28.2 %copy-start = (bf16[16,3,2,64,128]{4,3,2,1,0:T(8,128)(2,1)S(1)}, bf16[16,3,2,64,128]{4,3,2,1,0:T(8,128)(2,1)}, u32[]{:S(2)}) copy-start(bf16[16,3,2,64,128]{4,3,2,1,0:T(8,128)(2,1)} %param.4) | copy-start | bytes 4718596
  6.5 28.2 %copy-start.2 = (bf16[3,2,64,128]{3,2,1,0:T(8,128)(2,1)S(1)}, bf16[3,2,64,128]{3,2,1,0:T(8,128)(2,1)}, u32[]{:S(2)}) copy-start(bf16[3,2,64,128]{3,2,1,0:T(8,128)(2,1)} %param.5) | copy-start | bytes 294916
  6.5 8.2 %copy-start.3 = (f32[128,64]{0,1:T(8,128)S(1)}, f32[128,64]{0,1:T(8,128)}, u32[]{:S(2)}) copy-start(f32[128,64]{0,1:T(8,128)} %param.6) | copy-start | bytes 98308
  6.5 214.7 %all-gather.3.cloned.1.call-start = ((), (), s32[]{:S(2)}) async-start(), calls=%async_computation.1 | async-start | bytes 16842752 | tf_op jit(solution)/shard_map/all_gather | solution.py:108
  9.4 21.6 %collective-permute-start = (bf16[17,3,1,64,128]{4,3,2,1,0:T(8,128)(2,1)}, bf16[17,3,1,64,128]{4,3,2,1,0:T(8,128)(2,1)S(1)}, u32[]{:S(2)}, u32[]{:S(2)}) collective-permute-start(bf16[17,3,1,64,128]{4,3,2,1,0:T(8,128)(2,1)} %get-tuple-element.20), channel_id=1, source_target_pairs={{0,8},{8,16},{16,24},{24,32},{32,40},{40,48},{48,56},{56,64},{64,7... | collective-permute-start | bytes 2506760 | tf_op jit(solution)/shard_map/ppermute | solution.py:14
  13.5 21.3 %collective-permute-start.1 = (bf16[17,3,1,64,128]{4,3,2,1,0:T(8,128)(2,1)}, bf16[17,3,1,64,128]{4,3,2,1,0:T(8,128)(2,1)S(1)}, u32[]{:S(2)}, u32[]{:S(2)}) collective-permute-start(bf16[17,3,1,64,128]{4,3,2,1,0:T(8,128)(2,1)} %get-tuple-element.21), channel_id=1, source_target_pairs={{8,0},{16,8},{24,16},{32,24},{40,32},{48,40},{56,48},{64,56},{72,6... | collective-permute-start | bytes 2506760 | tf_op jit(solution)/shard_map/ppermute | solution.py:17
  227.8 5.2 %copy-start.1 = (f32[6144,128]{1,0:T(8,128)S(1)}, f32[6144,128]{1,0:T(8,128)}, u32[]{:S(2)}) copy-start(f32[6144,128]{1,0:T(8,128)} %copy.24) | copy-start | bytes 9437188
Sparse Core Ops, SparseCore 0:
  92.3 128.8 all-gather.2
